TPU v7x, 256 devices: a whole 4x4x8 slice. The times are simulated.
256 devices in a mesh: cfg: 2 (over core), seq: 32 (over y, z), blk: 4 (over x).
Axes of the slice: x: 4, y: 4, z: 8, core: 2. Of those that a mesh axis runs over, the one named last changes fastest.
Arguments:
- queries: bfloat16 [2, 12288, 1536], P('cfg', 'seq', 'blk'), may hold values from -20 to 20
- keys: bfloat16 [2, 12288, 1536], P('cfg', 'seq', 'blk'), may hold values from -20 to 20
- values: bfloat16 [2, 12288, 1536], P('cfg', 'seq', 'blk'), may hold values from -6 to 6
- residual: bfloat16 [2, 12288, 1536], P('cfg', 'seq'), may hold values from -6 to 6
- w_out: bfloat16 [1536, 1536], P('blk'), may hold values from -0.15625 to 0.15625
- w_up: bfloat16 [1536, 6144], P(None, 'blk'), may hold values from -0.15625 to 0.15625
- w_down: bfloat16 [6144, 1536], P('blk'), may hold values from -0.078125 to 0.078125
- modulation: float32 [3, 4, 1536], replicated, may hold values from -3 to 3
- guide_scale: float32 [3], replicated, may hold values from 1.5 to 4
- slot_clip: int32 [12288], P('seq'), may hold values from 0 to 3, as said below
- owner: int32 [12288, 1], P('seq'), may hold values from 0 to 31; in each aligned block of 192 rows (0 to 191, 192 to 383, ...) at most 12 rows name the same one
Outputs:
- returned: bfloat16 [2, 12288, 1536], P('cfg', 'seq', 'blk')
Inputs may be any that keep to these rules, and one draw needn't show every extreme that they name: `slot_clip`: each device's block of 384 slots holds its live slots first and its padding slots, marked 3, last; live slots, counted block after block, are dealt to the clips in turn (the t-th live slot belongs to clip t mod 3), so each clip has 3584 live slots. In each aligned half-block of 192 slots no owner is named more than 12 times.
All inputs are finite; a program needn't handle non-finite values.
Results may differ from a plain program's by a relative error of at most 0.017.
Values may be sent and summed in bfloat16 or wider, within the bound.
A program may use at most 128 MiB of HBM per device.

v0:
```python
import math
import jax
import jax.numpy as jnp
from jax import lax
from jax.sharding import PartitionSpec as P

D = 1536
HEAD_DIM = 128
CLIPS = 3
NEG_FILL = -1e30


def swapped(value, axis, bit):
    mask = 2**bit
    pairs = [(source, source ^ mask) for source in range(lax.axis_size(axis))]
    return lax.ppermute(value, axis, pairs)


def shards(
    queries, keys, values, residual, w_out, w_up, w_down, modulation, guide_scale, slot_clip, owner
):
    query_here = queries[0]
    slots, width = query_here.shape
    heads_here = width // HEAD_DIM
    factor = 1.0 / math.sqrt(HEAD_DIM)
    live = slot_clip < CLIPS
    query_heads = query_here.reshape(slots, heads_here, HEAD_DIM)

    def absorb_block(carry, key_block, value_block, clip_block):
        count = key_block.shape[0]
        kept = (clip_block[None, :] == slot_clip[:, None]) & live[:, None]
        best, total, accum = carry
        key_heads = key_block.reshape(count, heads_here, HEAD_DIM)
        value_heads = value_block.reshape(count, heads_here, HEAD_DIM)
        scores = (
            jnp.einsum("qhd,khd->hqk", query_heads, key_heads, preferred_element_type=jnp.float32)
            * factor
        )
        scores = jnp.where(kept[None], scores, NEG_FILL)
        new_best = jnp.maximum(best, jnp.max(scores, axis=-1))
        fade = jnp.exp(best - new_best)
        probs = jnp.exp(scores - new_best[..., None])
        total = total * fade + jnp.sum(probs, axis=-1)
        added = jnp.einsum(
            "hqk,khd->qhd",
            probs.astype(jnp.bfloat16),
            value_heads,
            preferred_element_type=jnp.float32,
        )
        accum = accum * jnp.transpose(fade)[:, :, None] + added
        return (new_best, total, accum)

    def absorb(carry, piece):
        key_piece, value_piece, clip_piece = piece
        count = key_piece.shape[0]
        step_rows = next(
            (size_b for size_b in (512, 384, 256, 128) if count % size_b == 0 and count > size_b),
            count,
        )
        if step_rows == count:
            return absorb_block(carry, key_piece, value_piece, clip_piece)
        blocks = count // step_rows

        def scan_step(state, block_items):
            return (absorb_block(state, block_items[0], block_items[1], block_items[2]), None)

        stacked = (
            key_piece.reshape(blocks, step_rows, width),
            value_piece.reshape(blocks, step_rows, width),
            clip_piece.reshape(blocks, step_rows),
        )
        carry_out, unused = lax.scan(scan_step, carry, stacked)
        return carry_out

    start_state = (
        jnp.full((heads_here, slots), NEG_FILL, jnp.float32),
        jnp.zeros((heads_here, slots), jnp.float32),
        jnp.zeros((slots, heads_here, HEAD_DIM), jnp.float32),
    )
    best, total, accum = absorb(
        start_state,
        (
            lax.all_gather(keys[0], "seq", axis=0, tiled=True),
            lax.all_gather(values[0], "seq", axis=0, tiled=True),
            lax.all_gather(slot_clip, "seq", axis=0, tiled=True),
        ),
    )
    attended = (accum / jnp.transpose(total)[:, :, None]).reshape(slots, width)
    attended = jnp.where(live[:, None], attended, 0.0).astype(jnp.bfloat16)
    partial_out = jnp.dot(attended, w_out, preferred_element_type=jnp.float32)
    selector = (slot_clip[:, None] == jnp.arange(CLIPS, dtype=jnp.int32)[None, :]).astype(
        jnp.float32
    )
    row_mod = jnp.dot(
        selector, modulation.reshape(CLIPS, 4 * D), precision=lax.Precision.HIGHEST
    ).reshape(slots, 4, D)
    columns = D // lax.axis_size("blk")
    col_start = lax.axis_index("blk") * columns
    mod_cols = lax.dynamic_slice_in_dim(row_mod, col_start, columns, 2)
    projected = lax.psum(partial_out.astype(jnp.bfloat16), "blk").astype(jnp.float32)
    mixed = residual[0].astype(jnp.float32) + row_mod[:, 0] * projected
    centre = mixed - jnp.mean(mixed, axis=-1, keepdims=True)
    spread = jnp.mean(centre * centre, axis=-1, keepdims=True)
    normed = (centre * lax.rsqrt(spread + 1e-06) * (1.0 + row_mod[:, 2]) + row_mod[:, 1]).astype(
        jnp.bfloat16
    )
    mixed_cols = lax.dynamic_slice_in_dim(mixed, col_start, columns, 1)
    hidden = jax.nn.gelu(
        jnp.dot(normed, w_up, preferred_element_type=jnp.float32), approximate=True
    ).astype(jnp.bfloat16)
    terms = jnp.dot(hidden, w_down, preferred_element_type=jnp.float32)
    summed = lax.psum_scatter(
        terms.astype(jnp.bfloat16), "blk", scatter_dimension=1, tiled=True
    ).astype(jnp.float32)
    block_out = (mixed_cols + mod_cols[:, 3] * summed).astype(jnp.bfloat16)
    half_len = slots // 2
    side = lax.axis_index("cfg")
    partner = swapped(block_out, "cfg", 0)
    cond_all = jnp.where(side == 0, block_out, partner)
    uncond_all = jnp.where(side == 0, partner, block_out)
    cond_rows = lax.dynamic_slice_in_dim(cond_all, side * half_len, half_len, 0)
    uncond_rows = lax.dynamic_slice_in_dim(uncond_all, side * half_len, half_len, 0)
    clip_half = lax.dynamic_slice_in_dim(slot_clip, side * half_len, half_len, 0)
    clip_pick = (clip_half[:, None] == jnp.arange(CLIPS, dtype=jnp.int32)[None, :]).astype(
        jnp.float32
    )
    strength = jnp.sum(clip_pick * guide_scale[None, :], axis=1)
    cond_float = cond_rows.astype(jnp.float32)
    uncond_float = uncond_rows.astype(jnp.float32)
    guided = uncond_float + strength[:, None] * (cond_float - uncond_float)
    guided = jnp.where((clip_half < CLIPS)[:, None], guided, 0.0).astype(jnp.bfloat16)
    seq_count = lax.axis_size("seq")
    capacity = max(2, slots // seq_count)
    owner_half = lax.dynamic_slice_in_dim(owner[:, 0], side * half_len, half_len, 0)
    owner_hot = (owner_half[:, None] == jnp.arange(seq_count, dtype=jnp.int32)[None, :]).astype(
        jnp.int32
    )
    rank = jnp.sum((jnp.cumsum(owner_hot, axis=0) - owner_hot) * owner_hot, axis=1)
    target = owner_half * capacity + rank
    placing = (
        jnp.arange(seq_count * capacity, dtype=jnp.int32)[:, None] == target[None, :]
    ).astype(jnp.bfloat16)
    outgoing = jnp.dot(placing, guided, preferred_element_type=jnp.float32).astype(jnp.bfloat16)
    outgoing = outgoing.reshape(seq_count, capacity, columns)
    arrived = lax.all_to_all(outgoing, "seq", split_axis=0, concat_axis=0, tiled=True)
    return arrived.reshape(1, seq_count * capacity, columns)


def solution(mesh):
    placed = (
        P("cfg", "seq", "blk"),
        P("cfg", "seq", "blk"),
        P("cfg", "seq", "blk"),
        P("cfg", "seq", None),
        P("blk", None),
        P(None, "blk"),
        P("blk", None),
        P(),
        P(),
        P("seq"),
        P("seq", None),
    )
    return jax.shard_map(
        shards, mesh=mesh, in_specs=placed, out_specs=P("cfg", "seq", "blk"), check_vma=False
    )
```

profile of v0, /device:TPU:32, one launch (start us, length us, event | category | flops | bytes accessed | tf_op | source)
XLA Modules:
  0.0 713.3 jit_solution(6214231156440288934)
XLA Ops:
  10.8 48.8 %all-gather.2 = s32[32,1,384]{2,1,0:T(1,128)S(1)} all-gather(s32[1,1,384]{2,1,0:T(1,128)S(1)} %reshape.132), channel_id=1, replica_groups=mesh['cfg'=2,'seq'=32,'blk'=4] {'seq'}, dimensions={0}, use_global_device_ids=true | all-gather | bytes 50688 | tf_op jit(solution)/shard_map/all_gather | solution.py:85
  61.6 53.0 %all-gather.6.cloned.1.call-done = bf16[1,12288,384]{2,1,0:T(8,128)(2,1)} async-done(((bf16[1,384,384]{2,1,0:T(8,128)(2,1)}), bf16[1,12288,384]{2,1,0:T(8,128)(2,1)}) %all-gather.6.cloned.1.call-update) | async-done | bytes 9437200 | tf_op jit(solution)/shard_map/all_gather | solution.py:83
  114.6 103.2 %all-gather.8.cloned.1.call-done = bf16[1,12288,384]{2,1,0:T(8,128)(2,1)} async-done(((bf16[1,384,384]{2,1,0:T(8,128)(2,1)}), bf16[1,12288,384]{2,1,0:T(8,128)(2,1)}) %all-gather.8.cloned.1.call-update) | async-done | bytes 9437200 | tf_op jit(solution)/shard_map/all_gather | solution.py:84
  217.8 360.1 %while.15 = (s32[]{:T(128)}, f32[3,384]{1,0:T(4,128)S(1)}, f32[3,384]{1,0:T(4,128)}, f32[384,3,128]{0,2,1:T(8,128)}, s32[24,512]{1,0:T(8,128)}, /*index=5*/s32[3...) while((s32[]{:T(128)}, f32[3,384]{1,0:T(4,128)S(1)}, ...), condition=%wide.region_6.7_spmd.clone, body=%wide.region_3.6_spmd.clone.sunk | while | flops 309320448 | bytes 14176349 | solution.py:72
  243.4 2.9 fusion.94
  258.4 2.9 fusion.94
  273.4 2.9 fusion.94
  288.4 2.9 fusion.94
  303.4 2.9 fusion.94
  318.5 2.9 fusion.94
  333.5 2.9 fusion.94
  348.5 2.9 fusion.94
  363.5 2.9 fusion.94
  378.5 2.9 fusion.94
  393.5 2.9 fusion.94
  408.5 2.9 fusion.94
  423.6 2.9 fusion.94
  438.6 2.9 fusion.94
  453.6 2.9 fusion.94
  468.6 2.9 fusion.94
  483.6 2.9 fusion.94
  498.6 2.9 fusion.94
  513.7 2.9 fusion.94
  528.7 2.9 fusion.94
  543.7 2.9 fusion.94
  558.7 2.9 fusion.94
  573.7 2.9 fusion.94
  581.7 6.4 fusion.56
  588.2 44.1 %all-reduce.3.cloned.1.call-done = bf16[384,1536]{1,0:T(8,128)(2,1)} async-done(((bf16[384,1536]{1,0:T(8,128)(2,1)}), bf16[384,1536]{1,0:T(8,128)(2,1)}) %all-reduce.3.cloned.1.call-update) | async-done | bytes 1179664 | tf_op jit(solution)/shard_map/psum | solution.py:100
  635.4 10.1 %convolution_convert_fusion = bf16[384,1536]{1,0:T(8,128)(2,1)} fusion(bf16[1536,1536]{1,0:T(8,128)(2,1)} %param.19, bf16[1536,1536]{1,0:T(8,128)(2,1)} %param.18, f32[384,4,1536]{2,0,1:T(8,128)} %fusion.56, f32[384,1536]{1,0:T(8,128)S(1)} %get-tuple-element.158, f32[384]{0:T(512)S(1)} %add_rsqrt_fusion, f32[384]{0:T(512)S(1)} %broadcast_multiply_fusion), kind=kOutput, calls=%fused_computation.24 | convolution fusion | flops 3633315840 | bytes 17697792 | tf_op jit(solution)/shard_map/dot_general | solution.py:111
  652.9 22.6 %reduce-scatter.4.cloned.1.call-done = bf16[384,384]{1,0:T(8,128)(2,1)} async-done(((bf16[1536,384]{1,0:T(8,128)(2,1)}), bf16[384,384]{1,0:T(8,128)(2,1)}) %reduce-scatter.4.cloned.1.call-update) | async-done | bytes 294928
  680.8 25.2 %all_to_all.5 = bf16[32,12,384]{2,1,0:T(8,128)(2,1)S(1)} all-to-all(bf16[32,12,384]{2,1,0:T(8,128)(2,1)S(1)} %reshape.124), channel_id=1, replica_groups=mesh['cfg'=2,'seq'=32,'blk'=4] {'seq'}, dimensions={0} | all-to-all | bytes 589824 | tf_op jit(solution)/shard_map/all_to_all | solution.py:145
  (439 shorter events, 319.5 us)
Async XLA Ops:
  6.5 573.2 %copy-start = (bf16[384,1536]{1,0:T(8,128)(2,1)S(1)}, bf16[384,1536]{1,0:T(8,128)(2,1)}, u32[]{:S(2)}) copy-start(bf16[384,1536]{1,0:T(8,128)(2,1)} %param.17) | copy-start | bytes 3538948
  6.5 108.1 %all-gather.6.cloned.1.call-start = ((), (), s32[]{:S(2)}) async-start(), calls=%async_computation.3 | async-start | bytes 9732096 | tf_op jit(solution)/shard_map/all_gather | solution.py:83
  7.3 210.5 %all-gather.8.cloned.1.call-start = ((), (), s32[]{:S(2)}) async-start(), calls=%async_computation.4 | async-start | bytes 9732096 | tf_op jit(solution)/shard_map/all_gather | solution.py:84
  8.0 624.2 %all-reduce.3.cloned.1.call-start = ((), (), s32[]{:S(2)}) async-start(), calls=%async_computation.2 | async-start | bytes 2359296 | tf_op jit(solution)/shard_map/psum | solution.py:100
  228.6 2.7 copy-start.1
  243.4 2.9 copy-start.1
  258.4 2.9 copy-start.1
  273.4 2.9 copy-start.1
  288.4 2.9 copy-start.1
  303.4 2.9 copy-start.1
  318.5 2.9 copy-start.1
  333.5 2.9 copy-start.1
  348.5 2.9 copy-start.1
  363.5 2.9 copy-start.1
  378.5 2.9 copy-start.1
  393.5 2.9 copy-start.1
  408.5 2.9 copy-start.1
  423.6 2.9 copy-start.1
  438.6 2.9 copy-start.1
  453.6 2.9 copy-start.1
  468.6 2.9 copy-start.1
  483.6 2.9 copy-start.1
  498.6 2.9 copy-start.1
  513.7 2.9 copy-start.1
  528.7 2.9 copy-start.1
  543.7 2.9 copy-start.1
  558.7 2.9 copy-start.1
  573.7 2.9 copy-start.1
  579.0 2.6 copy-start.4
  581.6 93.9 %reduce-scatter.4.cloned.1.call-start = ((), (), s32[]{:S(2)}) async-start(), calls=%async_computation.5 | async-start | bytes 1474560
  652.9 27.4 %copy-start.7 = (pred[192]{0:T(512)(128)(4,1)S(1)}, pred[192]{0:T(512)(128)(4,1)}, u32[]{:S(2)}) copy-start(pred[192]{0:T(512)(128)(4,1)} %get-tuple-element.155) | copy-start | bytes 580
  678.7 1.7 collective-permute-start
  (50 other events, 36.0 us)
Sparse Core Ops, SparseCore 0:
  9.9 104.6 all-gather.5
  117.2 100.5 all-gather.7
  581.8 50.4 all-reduce.2
  648.0 27.5 reduce-scatter.3
where the time goes:
time: 720 us; the launch traced here: 713 us
  waiting for transfers between devices  225 us (31%)
  local copies, waits for them, and re-layouts  160 us (22%)
  matrix products  146 us (20%)
  other arithmetic  94.2 us (13%)
  blocking collectives  74 us (10%)
  between operations  13.3 us (2%)
    dynamic_slice x96, local copies, waits for them, and re-layouts, absorb(): carry_out, unused = lax.scan(scan_step, carry, stacked)  133 us
    all_gather x1, waiting for transfers between devices, shards(): lax.all_gather(values[0], 'seq', axis=0, tiled=True)  103 us
    dot_general x24, matrix products, absorb_block(): jnp.einsum('hqk,khd->qhd', probs.astype(jnp.bfloat16), value_heads, prefe...  69.4 us
    dot_general x24, matrix products, absorb_block(): jnp.einsum('qhd,khd->hqk', query_heads, key_heads, preferred_element_type...  57.5 us
    all_gather x1, waiting for transfers between devices, shards(): lax.all_gather(keys[0], 'seq', axis=0, tiled=True)  53 us
    all_gather x1, blocking collectives, shards(): lax.all_gather(slot_clip, 'seq', axis=0, tiled=True)  48.8 us
    psum x1, waiting for transfers between devices, shards(): lax.psum(partial_out.astype(jnp.bfloat16), 'blk').astype(jnp.float32)  44.1 us
    and x24, other arithmetic, absorb_block(): kept = (clip_block[None, :] == slot_clip[:, None]) & live[:, None]  37.3 us
  transfers between devices with their start and end apart: 5, of which 5 were waited for; matrix products, arithmetic and copies ran while one was open for 2% of the time, Pallas kernels for 0%

commit v1 on v0

--- a/solution.py
+++ b/solution.py
@@ -8,6 +8,13 @@
 HEAD_DIM = 128
 CLIPS = 3
 NEG_FILL = -1e30
+
+
+def exchange_gather(x, name, d):
+    peers = lax.axis_size(name)
+    blocks = jnp.stack([x for _ in range(peers)])
+    blocks = lax.all_to_all(blocks, name, split_axis=0, concat_axis=0)
+    return jnp.concatenate(blocks, axis=d)
 
 
 def swapped(value, axis, bit):
@@ -81,7 +88,7 @@
         start_state,
         (
             lax.all_gather(keys[0], "seq", axis=0, tiled=True),
-            lax.all_gather(values[0], "seq", axis=0, tiled=True),
+            exchange_gather(values[0], "seq", 0),
             lax.all_gather(slot_clip, "seq", axis=0, tiled=True),
         ),
     )

time: 720 us -> 834 us (1.16)
  blocking collectives: 74 us -> 326 us
  waiting for transfers between devices: 225 us -> 69.1 us
  starting transfers between devices: 0.21 us -> 11.9 us
    all_gather x1, blocking collectives: 48.8 us -> 301 us  [shards(): lax.all_gather(slot_clip, 'seq', axis=0, tiled=True)]
    all_gather x1 -> x0, waiting for transfers between devices: 103 us -> none  [shards(): lax.all_gather(values[0], 'seq', axis=0, tiled=True)]
    all_gather x1, waiting for transfers between devices: 53 us -> 0.01 us  [shards(): lax.all_gather(keys[0], 'seq', axis=0, tiled=True)]
    all_to_all x0 -> x1, starting transfers between devices: none -> 11.5 us  [exchange_gather(): blocks = lax.all_to_all(blocks, name, split_axis=0, concat_axis=0)]
    unnamed x5 -> x4, waiting for transfers between devices: 24.1 us -> 22.7 us
  transfers between devices with their start and end apart: 5 -> 5, of which waited for: 5 -> 3; matrix products, arithmetic and copies ran while one was open for 2% -> 2% of each run, Pallas kernels for 0% -> 0%
where the time goes in v1:
time: 834 us; the launch traced here: 827 us
  blocking collectives  326 us (39%)
  local copies, waits for them, and re-layouts  165 us (20%)
  matrix products  147 us (18%)
  other arithmetic  95 us (11%)
  waiting for transfers between devices  69.1 us (8%)
  between operations  13.3 us (2%)
  starting transfers between devices  11.9 us (1%)
    all_gather x1, blocking collectives, shards(): lax.all_gather(slot_clip, 'seq', axis=0, tiled=True)  301 us
    dynamic_slice x96, local copies, waits for them, and re-layouts, absorb(): carry_out, unused = lax.scan(scan_step, carry, stacked)  133 us
    dot_general x24, matrix products, absorb_block(): jnp.einsum('hqk,khd->qhd', probs.astype(jnp.bfloat16), value_heads, prefe...  69.1 us
    dot_general x24, matrix products, absorb_block(): jnp.einsum('qhd,khd->hqk', query_heads, key_heads, preferred_element_type...  57.6 us
    psum x1, waiting for transfers between devices, shards(): lax.psum(partial_out.astype(jnp.bfloat16), 'blk').astype(jnp.float32)  45.6 us
    and x24, other arithmetic, absorb_block(): kept = (clip_block[None, :] == slot_clip[:, None]) & live[:, None]  37.6 us
    transpose x24, other arithmetic, absorb_block(): accum = accum * jnp.transpose(fade)[:, :, None] + added  31 us
    all_to_all x1, blocking collectives, shards(): lax.all_to_all(outgoing, 'seq', split_axis=0, concat_axis=0, tiled=True)  25.2 us
  transfers between devices with their start and end apart: 5, of which 3 were waited for; matrix products, arithmetic and copies ran while one was open for 2% of the time, Pallas kernels for 0%

profile of v1, /device:TPU:32, one launch (start us, length us, event | category | flops | bytes accessed | tf_op | source)
XLA Modules:
  0.0 827.5 jit_solution(2736977308631086339)
XLA Ops:
  6.5 6.2 stack.3
  12.7 11.5 %all-to-all-start = ((bf16[32,384,384]{2,1,0:T(8,128)(2,1)}), bf16[32,384,384]{2,1,0:T(8,128)(2,1)}, u32[]{:S(2)}, u32[]{:S(2)}) async-start(bf16[32,384,384]{2,1,0:T(8,128)(2,1)} %stack.3), calls=%async_computation | async-start | bytes 18874368 | tf_op jit(solution)/shard_map/all_to_all | solution.py:16
  26.9 300.7 %all-gather.1 = s32[32,1,384]{2,1,0:T(1,128)S(1)} all-gather(s32[1,1,384]{2,1,0:T(1,128)S(1)} %reshape.127), channel_id=1, replica_groups=mesh['cfg'=2,'seq'=32,'blk'=4] {'seq'}, dimensions={0}, use_global_device_ids=true | all-gather | bytes 50688 | tf_op jit(solution)/shard_map/all_gather | solution.py:92
  329.5 359.7 %while.15 = (s32[]{:T(128)}, f32[3,384]{1,0:T(4,128)S(1)}, f32[3,384]{1,0:T(4,128)}, f32[384,3,128]{0,2,1:T(8,128)}, s32[24,512]{1,0:T(8,128)}, /*index=5*/s32[3...) while((s32[]{:T(128)}, f32[3,384]{1,0:T(4,128)S(1)}, ...), condition=%wide.region_6.7_spmd.clone, body=%wide.region_3.6_spmd.clone.sunk | while | flops 309320448 | bytes 14176349 | solution.py:79
  355.1 2.9 fusion.94
  370.1 2.9 fusion.94
  385.1 2.9 fusion.94
  400.1 2.9 fusion.94
  415.1 2.9 fusion.94
  430.1 2.9 fusion.94
  445.1 2.9 fusion.94
  460.0 2.9 fusion.94
  475.0 2.9 fusion.94
  490.0 2.9 fusion.94
  505.0 2.9 fusion.94
  520.0 2.9 fusion.94
  535.0 2.9 fusion.94
  550.0 2.9 fusion.94
  565.0 2.9 fusion.94
  580.0 2.9 fusion.94
  595.0 2.9 fusion.94
  610.0 2.9 fusion.94
  625.0 2.9 fusion.94
  640.0 2.9 fusion.94
  655.0 2.9 fusion.94
  670.0 2.9 fusion.94
  685.0 2.9 fusion.94
  693.1 7.1 fusion.56
  700.3 45.6 %all-reduce.3.cloned.1.call-done = bf16[384,1536]{1,0:T(8,128)(2,1)} async-done(((bf16[384,1536]{1,0:T(8,128)(2,1)}), bf16[384,1536]{1,0:T(8,128)(2,1)}) %all-reduce.3.cloned.1.call-update) | async-done | bytes 1179664 | tf_op jit(solution)/shard_map/psum | solution.py:107
  749.0 10.1 %convolution_convert_fusion = bf16[384,1536]{1,0:T(8,128)(2,1)} fusion(bf16[1536,1536]{1,0:T(8,128)(2,1)} %param.19, bf16[1536,1536]{1,0:T(8,128)(2,1)} %param.18, f32[384,4,1536]{2,0,1:T(8,128)} %fusion.56, f32[384,1536]{1,0:T(8,128)S(1)} %get-tuple-element.158, f32[384]{0:T(512)S(1)} %add_rsqrt_fusion, f32[384]{0:T(512)S(1)} %broadcast_multiply_fusion), kind=kOutput, calls=%fused_computation.24 | convolution fusion | flops 3633315840 | bytes 17697792 | tf_op jit(solution)/shard_map/dot_general | solution.py:118
  767.2 22.0 %reduce-scatter.4.cloned.1.call-done = bf16[384,384]{1,0:T(8,128)(2,1)} async-done(((bf16[1536,384]{1,0:T(8,128)(2,1)}), bf16[384,384]{1,0:T(8,128)(2,1)}) %reduce-scatter.4.cloned.1.call-update) | async-done | bytes 294928
  795.0 25.2 %all_to_all.10 = bf16[32,12,384]{2,1,0:T(8,128)(2,1)S(1)} all-to-all(bf16[32,12,384]{2,1,0:T(8,128)(2,1)S(1)} %reshape.121), channel_id=1, replica_groups=mesh['cfg'=2,'seq'=32,'blk'=4] {'seq'}, dimensions={0} | all-to-all | bytes 589824 | tf_op jit(solution)/shard_map/all_to_all | solution.py:152
  (437 shorter events, 319.1 us)
Async XLA Ops:
  6.5 684.5 %copy-start = (bf16[384,1536]{1,0:T(8,128)(2,1)S(1)}, bf16[384,1536]{1,0:T(8,128)(2,1)}, u32[]{:S(2)}) copy-start(bf16[384,1536]{1,0:T(8,128)(2,1)} %param.17) | copy-start | bytes 3538948
  12.7 12.4 %copy-start.2 = (bf16[1,384,384]{2,1,0:T(8,128)(2,1)S(1)}, bf16[1,384,384]{2,1,0:T(8,128)(2,1)}, u32[]{:S(2)}) copy-start(bf16[1,384,384]{2,1,0:T(8,128)(2,1)} %param.13) | copy-start | bytes 884740
  12.7 316.8 %all-to-all-start = ((bf16[32,384,384]{2,1,0:T(8,128)(2,1)}), bf16[32,384,384]{2,1,0:T(8,128)(2,1)}, u32[]{:S(2)}, u32[]{:S(2)}) async-start(bf16[32,384,384]{2,1,0:T(8,128)(2,1)} %stack.3), calls=%async_computation | async-start | bytes 18874368 | tf_op jit(solution)/shard_map/all_to_all | solution.py:16
  24.3 305.2 %all-gather.4.cloned.1.call-start = ((), (), s32[]{:S(2)}) async-start(), calls=%async_computation.4 | async-start | bytes 9732096 | tf_op jit(solution)/shard_map/all_gather | solution.py:90
  25.0 720.8 %all-reduce.3.cloned.1.call-start = ((), (), s32[]{:S(2)}) async-start(), calls=%async_computation.3 | async-start | bytes 2359296 | tf_op jit(solution)/shard_map/psum | solution.py:107
  340.3 2.7 copy-start.1
  355.1 2.9 copy-start.1
  370.1 2.9 copy-start.1
  385.1 2.9 copy-start.1
  400.1 2.9 copy-start.1
  415.1 2.9 copy-start.1
  430.1 2.9 copy-start.1
  445.0 2.9 copy-start.1
  460.0 2.9 copy-start.1
  475.0 2.9 copy-start.1
  490.0 2.9 copy-start.1
  505.0 2.9 copy-start.1
  520.0 2.9 copy-start.1
  535.0 2.9 copy-start.1
  550.0 2.9 copy-start.1
  565.0 2.9 copy-start.1
  580.0 2.9 copy-start.1
  595.0 2.9 copy-start.1
  610.0 2.9 copy-start.1
  625.0 2.9 copy-start.1
  640.0 2.9 copy-start.1
  655.0 2.9 copy-start.1
  670.0 2.9 copy-start.1
  685.0 2.9 copy-start.1
  690.3 2.8 copy-start.5
  692.9 96.3 %reduce-scatter.4.cloned.1.call-start = ((), (), s32[]{:S(2)}) async-start(), calls=%async_computation.5 | async-start | bytes 1474560
  792.3 1.7 collective-permute-start
  (49 other events, 33.4 us)
Sparse Core Ops, SparseCore 0:
  27.7 245.9 all-gather.3
  693.0 52.7 all-reduce.2
  761.6 27.5 reduce-scatter.3
